TPU v7x, 32 devices: a whole 2x2x4 slice. The times are simulated.
32 devices in a mesh: dp: 8 (over y, x, core), tensor: 4 (over z).
Axes of the slice: x: 2, y: 2, z: 4, core: 2. Of those that a mesh axis runs over, the one named last changes fastest.
Arguments:
- tokens: bfloat16 [4096, 4096], P(('dp', 'tensor')), may hold values from -120 to 120
- norm_gain: float32 [4096], replicated, may hold values from 0.5 to 1.5
- w_gate: bfloat16 [4096, 8192], P('dp', 'tensor'), may hold values from -0.09375 to 0.09375
- w_up: bfloat16 [4096, 8192], P('dp', 'tensor'), may hold values from -0.09375 to 0.09375
- probes: bfloat16 [4096, 2, 8192], P('dp', None, 'tensor'), may hold values from -0.09375 to 0.09375
- cotangent: bfloat16 [4096, 8192], P('dp', 'tensor'), may hold values from -6 to 6
Outputs:
- hvp: float32 [4096, 2, 8192], P('dp', None, 'tensor')
All inputs are finite; a program needn't handle non-finite values.
Results may differ from a plain program's by a relative error of at most 0.014.
Values may be sent and summed in bfloat16 or wider, within the bound.
A program may use at most 128 MiB of HBM per device.

v0:
```python
import math

import jax
import jax.numpy as jnp
from jax import lax
from jax.sharding import PartitionSpec as P


def normalize(tokens, norm_gain):
    values = tokens.astype(jnp.float32)
    inverse = lax.rsqrt(jnp.mean(values * values, axis=1, keepdims=True) + 1e-05)
    return (values * inverse * norm_gain).astype(jnp.bfloat16)


def curvature(gate_pre):
    logistic = jax.nn.sigmoid(gate_pre)
    return logistic * (1.0 - logistic) * (2.0 + gate_pre * (1.0 - 2.0 * logistic))


def per_device(tokens, norm_gain, w_gate, w_up, probes, cotangent):
    normed = lax.all_gather(normalize(tokens, norm_gain), "tensor", axis=0, tiled=True)
    row_count = normed.shape[0]
    local_depth, probe_count, local_units = probes.shape
    probe_width = probe_count * local_units

    def project(shard_piece):
        return jnp.dot(normed, shard_piece, preferred_element_type=jnp.float32)

    gate_pre = project(lax.all_gather(w_gate, "dp", axis=0, tiled=True))
    up_pre = project(lax.all_gather(w_up, "dp", axis=0, tiled=True))
    shard_piece = lax.all_gather(probes, "dp", axis=0, tiled=True)
    tangent = project(shard_piece.reshape(shard_piece.shape[0], probe_width))
    scale_factor = 1.0 / math.sqrt(row_count * lax.axis_size("dp"))
    weighting = cotangent.astype(jnp.float32) * curvature(gate_pre) * up_pre * scale_factor
    second = (weighting[:, None, :] * tangent.reshape(row_count, probe_count, local_units)).astype(
        jnp.bfloat16
    )
    second = second.reshape(row_count, probe_width)
    result = lax.psum_scatter(
        lax.dot_general(
            normed, second, (((0,), (0,)), ((), ())), preferred_element_type=jnp.float32
        ).astype(jnp.bfloat16),
        "dp",
        scatter_dimension=0,
        tiled=True,
    ).astype(jnp.float32)
    return result.reshape(local_depth, probe_count, local_units)


def solution(mesh):
    in_specs = (
        P(("dp", "tensor"), None),
        P(),
        P("dp", "tensor"),
        P("dp", "tensor"),
        P("dp", None, "tensor"),
        P("dp", "tensor"),
    )
    out_specs = P("dp", None, "tensor")
    return jax.shard_map(
        per_device, mesh=mesh, in_specs=in_specs, out_specs=out_specs, check_vma=False
    )
```

profile of v0, /device:TPU:0, one launch (start us, length us, event | category | flops | bytes accessed | tf_op | source)
XLA Modules:
  0.0 797.4 jit_solution(14628051146677067251)
XLA Ops:
  6.5 0.0 all-gather.5.cloned.1.call-start
  6.5 1.5 fusion.11
  8.1 2.5 fusion.13
  10.6 0.0 all-gather.5.cloned.1.call-update
  10.6 0.0 all-gather.7.cloned.1.call-start
  10.7 0.7 all-gather.7.cloned.1.call-update
  11.4 0.0 all-gather.9.cloned.1.call-start
  11.4 0.7 all-gather.9.cloned.1.call-update
  12.1 0.0 all-gather.11.cloned.1.call-start
  12.2 0.5 all-gather.11.cloned.1.call-update
  12.7 0.0 copy-start
  12.7 0.0 reduce-scatter.2.cloned.1.call-start
  12.7 81.5 %all-gather.5.cloned.1.call-done = bf16[512,4096]{1,0:T(8,128)(2,1)} async-done(((bf16[128,4096]{1,0:T(8,128)(2,1)}), bf16[512,4096]{1,0:T(8,128)(2,1)}) %all-gather.5.cloned.1.call-update) | async-done | bytes 4194320 | tf_op jit(solution)/shard_map/all_gather | solution.py:21
  94.2 90.1 %all-gather.7.cloned.1.call-done = bf16[4096,2048]{1,0:T(8,128)(2,1)} async-done(((bf16[512,2048]{1,0:T(8,128)(2,1)}), bf16[4096,2048]{1,0:T(8,128)(2,1)}) %all-gather.7.cloned.1.call-update) | async-done | bytes 16777232 | tf_op jit(solution)/shard_map/all_gather | solution.py:29
  184.4 14.9 %fusion.14 = f32[512,2048]{1,0:T(8,128)} fusion(bf16[512,4096]{1,0:T(8,128)(2,1)} %all-gather.5.cloned.1.call-done, bf16[4096,2048]{1,0:T(8,128)(2,1)} %all-gather.7.cloned.1.call-done), kind=kOutput, calls=%fused_computation.16 | convolution fusion | flops 8589934592 | bytes 25165824 | tf_op jit(solution)/shard_map/dot_general | solution.py:27
  199.3 76.8 %all-gather.9.cloned.1.call-done = bf16[4096,2048]{1,0:T(8,128)(2,1)} async-done(((bf16[512,2048]{1,0:T(8,128)(2,1)}), bf16[4096,2048]{1,0:T(8,128)(2,1)}) %all-gather.9.cloned.1.call-update) | async-done | bytes 16777232 | tf_op jit(solution)/shard_map/all_gather | solution.py:30
  276.0 0.0 copy-done
  276.0 17.0 %fusion.5 = f32[512,2048]{1,0:T(8,128)} fusion(f32[512,2048]{1,0:T(8,128)} %fusion.14, bf16[512,2048]{1,0:T(8,128)(2,1)S(1)} %copy-done, bf16[512,4096]{1,0:T(8,128)(2,1)} %all-gather.5.cloned.1.call-done, bf16[4096,2048]{1,0:T(8,128)(2,1)} %all-gather.9.cloned.1.call-done), kind=kOutput, calls=%fused_computation.8 | convolution fusion | flops 8604614656 | bytes 31457280 | tf_op jit(solution)/shard_map/dot_general | solution.py:27
  293.0 145.5 %all-gather.11.cloned.1.call-done = bf16[4096,2,2048]{2,1,0:T(2,128)(2,1)} async-done(((bf16[512,2,2048]{2,1,0:T(2,128)(2,1)}), bf16[4096,2,2048]{2,1,0:T(2,128)(2,1)}) %all-gather.11.cloned.1.call-update) | async-done | bytes 33554448 | tf_op jit(solution)/shard_map/all_gather | solution.py:31
  438.5 80.7 %copy.12 = bf16[4096,2,2048]{0,2,1:T(8,128)(2,1)} copy(bf16[4096,2,2048]{2,1,0:T(2,128)(2,1)} %all-gather.11.cloned.1.call-done) | data formatting | bytes 67108864 | tf_op jit(solution)/shard_map/reshape | solution.py:32
  519.2 24.2 %multiply_convert_fusion = bf16[512,2,2048]{2,0,1:T(8,128)(2,1)} fusion(f32[512,2048]{1,0:T(8,128)} %fusion.5, bf16[4096,2,2048]{0,2,1:T(8,128)(2,1)} %copy.12, bf16[512,4096]{1,0:T(8,128)(2,1)} %all-gather.5.cloned.1.call-done), kind=kOutput, calls=%fused_computation.3 | convolution fusion | flops 17184063488 | bytes 46137344 | tf_op jit(solution)/shard_map/dot_general | solution.py:27
  543.4 6.2 copy.11
  549.6 24.1 %convolution_convert_fusion = bf16[4096,4096]{1,0:T(8,128)(2,1)} fusion(bf16[512,4096]{1,0:T(8,128)(2,1)} %all-gather.5.cloned.1.call-done, bf16[512,4096]{0,1:T(8,128)(2,1)} %bitcast.21), kind=kOutput, calls=%fused_computation.2 | convolution fusion | flops 17196646400 | bytes 41943040 | tf_op jit(solution)/shard_map/dot_general | solution.py:40
  573.7 0.0 reduce-scatter.2.cloned.1.call-update
  573.7 205.6 %reduce-scatter.2.cloned.1.call-done = bf16[512,4096]{1,0:T(8,128)(2,1)} async-done(((bf16[4096,4096]{1,0:T(8,128)(2,1)}), bf16[512,4096]{1,0:T(8,128)(2,1)}) %reduce-scatter.2.cloned.1.call-update) | async-done | bytes 4194320 | tf_op jit(solution)/shard_map/reduce_scatter | solution.py:39
  779.4 11.5 %reshape.29 = f32[512,2,2048]{2,1,0:T(2,128)} reshape(bf16[512,4096]{1,0:T(8,128)(2,1)} %reduce-scatter.2.cloned.1.call-done) | data formatting | bytes 12582912 | tf_op jit(solution)/shard_map/reshape | solution.py:47
  (1 shorter events, 0.0 us)
Async XLA Ops:
  6.5 87.7 %all-gather.5.cloned.1.call-start = ((), (), s32[]{:S(2)}) async-start(), calls=%async_computation.1 | async-start | bytes 5242880 | tf_op jit(solution)/shard_map/all_gather | solution.py:21
  10.6 173.8 %all-gather.7.cloned.1.call-start = ((), (), s32[]{:S(2)}) async-start(), calls=%async_computation.2 | async-start | bytes 18874368 | tf_op jit(solution)/shard_map/all_gather | solution.py:29
  11.4 264.7 %all-gather.9.cloned.1.call-start = ((), (), s32[]{:S(2)}) async-start(), calls=%async_computation.3 | async-start | bytes 18874368 | tf_op jit(solution)/shard_map/all_gather | solution.py:30
  12.1 426.4 %all-gather.11.cloned.1.call-start = ((), (), s32[]{:S(2)}) async-start(), calls=%async_computation.4 | async-start | bytes 37748736 | tf_op jit(solution)/shard_map/all_gather | solution.py:31
  12.7 263.3 %copy-start = (bf16[512,2048]{1,0:T(8,128)(2,1)S(1)}, bf16[512,2048]{1,0:T(8,128)(2,1)}, u32[]{:S(2)}) copy-start(bf16[512,2048]{1,0:T(8,128)(2,1)} %param.11) | copy-start | bytes 6291460
  12.7 766.7 %reduce-scatter.2.cloned.1.call-start = ((), (), s32[]{:S(2)}) async-start(), calls=%async_computation.5 | async-start | bytes 37748736 | tf_op jit(solution)/shard_map/reduce_scatter | solution.py:39
Sparse Core Ops, SparseCore 0:
  10.7 83.4 all-gather.4
  96.1 88.2 all-gather.6
  186.3 89.7 all-gather.8
  277.8 160.6 all-gather.10
  573.9 205.4 reduce-scatter.1
where the time goes:
time: 800 us; the launch traced here: 797 us
  waiting for transfers between devices  601 us (75%)
  local copies, waits for them, and re-layouts  98.4 us (12%)
  matrix products  80.2 us (10%)
  between operations  13.2 us (2%)
    reduce_scatter x1, waiting for transfers between devices, per_device(): lax.psum_scatter(lax.dot_general(normed, second, (((0,), (0,)), ((), ()))...  206 us
    all_gather x1, waiting for transfers between devices, per_device(): shard_piece = lax.all_gather(probes, 'dp', axis=0, tiled=True)  145 us
    all_gather x1, waiting for transfers between devices, per_device(): gate_pre = project(lax.all_gather(w_gate, 'dp', axis=0, tiled=True))  90.1 us
    all_gather x1, waiting for transfers between devices, per_device(): lax.all_gather(normalize(tokens, norm_gain), 'tensor', axis=0, tiled=True)  81.5 us
    reshape x1, local copies, waits for them, and re-layouts, per_device(): tangent = project(shard_piece.reshape(shard_piece.shape[0], probe_width))  80.7 us
    all_gather x1, waiting for transfers between devices, per_device(): up_pre = project(lax.all_gather(w_up, 'dp', axis=0, tiled=True))  76.8 us
    dot_general x3, matrix products, project(): return jnp.dot(normed, shard_piece, preferred_element_type=jnp.float32)  56.1 us
    dot_general x1, matrix products, per_device(): lax.dot_general(normed, second, (((0,), (0,)), ((), ())), preferred_eleme...  24.1 us
  transfers between devices with their start and end apart: 5, of which 5 were waited for; matrix products, arithmetic and copies ran while one was open for 4% of the time, Pallas kernels for 0%

commit v1 on v0

--- a/solution.py
+++ b/solution.py
@@ -4,6 +4,9 @@
 import jax.numpy as jnp
 from jax import lax
 from jax.sharding import PartitionSpec as P
+
+LANES = 128
+PARTS = (3, 3, 2)
 
 
 def normalize(tokens, norm_gain):
@@ -17,7 +20,7 @@
     return logistic * (1.0 - logistic) * (2.0 + gate_pre * (1.0 - 2.0 * logistic))
 
 
-def per_device(tokens, norm_gain, w_gate, w_up, probes, cotangent):
+def gather_weights(tokens, norm_gain, w_gate, w_up, probes, cotangent):
     normed = lax.all_gather(normalize(tokens, norm_gain), "tensor", axis=0, tiled=True)
     row_count = normed.shape[0]
     local_depth, probe_count, local_units = probes.shape
@@ -47,6 +50,75 @@
     return result.reshape(local_depth, probe_count, local_units)
 
 
+def gather_tokens(tokens, norm_gain, w_gate, w_up, probes, cotangent):
+    ways = lax.axis_size("dp")
+    local_depth, probe_count, local_units = probes.shape
+    depth = local_depth * ways
+    units = local_units // ways
+    group = cotangent.shape[0]
+
+    def swap(blocks):
+        return lax.all_to_all(jnp.stack(blocks), "dp", 0, 0, tiled=True)
+
+    def columns(array, j, base=0):
+        return array[:, base + j * units : base + (j + 1) * units]
+
+    own = lax.all_gather(normalize(tokens, norm_gain), "tensor", axis=0, tiled=True)
+
+    pair = swap(
+        [jnp.concatenate([columns(w_gate, j), columns(w_up, j)], axis=1) for j in range(ways)]
+    ).reshape(depth, 2 * units)
+    cot = swap([columns(cotangent, j) for j in range(ways)])
+    flat = probes.reshape(local_depth, probe_count * local_units)
+    directions = swap(
+        [
+            jnp.concatenate(
+                [columns(flat, j, p * local_units) for p in range(probe_count)], axis=1
+            )
+            for j in range(ways)
+        ]
+    ).reshape(depth, probe_count * units)
+
+    scale_factor = 1.0 / math.sqrt(group * ways)
+    total = None
+    start = 0
+    for part in PARTS:
+        stop = start + group * part // sum(PARTS)
+        gathered = lax.all_gather(own[start:stop], "dp", axis=0, tiled=True)
+        if total is not None:
+            gathered, total = lax.optimization_barrier((gathered, total))
+        pre = jnp.dot(gathered, pair, preferred_element_type=jnp.float32)
+        tangent = jnp.dot(gathered, directions, preferred_element_type=jnp.float32)
+        here = cot[:, start:stop].reshape(-1, units).astype(jnp.float32)
+        weighting = here * curvature(pre[:, :units]) * pre[:, units:] * scale_factor
+        second = jnp.concatenate(
+            [
+                (weighting * columns(tangent, p)).astype(jnp.bfloat16)
+                for p in range(probe_count)
+            ],
+            axis=1,
+        )
+        term = lax.dot_general(
+            gathered, second, (((0,), (0,)), ((), ())), preferred_element_type=jnp.float32
+        )
+        total = term if total is None else total + term
+        start = stop
+
+    result = total.astype(jnp.bfloat16).reshape(ways, local_depth, probe_count * units)
+    result = lax.all_to_all(result, "dp", 0, 0, tiled=True)
+    flat = jnp.concatenate(
+        [columns(result[j], p) for p in range(probe_count) for j in range(ways)], axis=1
+    )
+    return flat.reshape(local_depth, probe_count, local_units).astype(jnp.float32)
+
+
+def per_device(tokens, norm_gain, w_gate, w_up, probes, cotangent):
+    ways = lax.axis_size("dp")
+    wide = w_gate.shape[1] % (ways * LANES) == 0 and cotangent.shape[0] % sum(PARTS) == 0
+    plan = gather_tokens if wide else gather_weights
+    return plan(tokens, norm_gain, w_gate, w_up, probes, cotangent)
+
+
 def solution(mesh):
     in_specs = (
         P(("dp", "tensor"), None),

time: 800 us -> 511 us (0.64)
  waiting for transfers between devices: 601 us -> 251 us
  blocking collectives: 0 us -> 51.6 us
  local copies, waits for them, and re-layouts: 98.4 us -> 55.6 us
  other arithmetic: 4.05 us -> 25.2 us
  matrix products: 80.2 us -> 95.3 us
  starting transfers between devices: 0.16 us -> 13.4 us
    all_gather x4, waiting for transfers between devices: 394 us -> 111 us  [the longest x1 83.6 us: gather_tokens(): lax.all_gather(normalize(tokens, norm_gain), 'tensor', axis=0, tiled=True)]
    reduce_scatter x1 -> x0, waiting for transfers between devices: 206 us -> none  [per_device(): lax.psum_scatter(lax.dot_general(normed, second, (((0,), (0,)), ((), ()))...]
    all_to_all x0 -> x3, waiting for transfers between devices: none -> 139 us  [swap(): return lax.all_to_all(jnp.stack(blocks), 'dp', 0, 0, tiled=True)]
    reshape x2 -> x0, local copies, waits for them, and re-layouts: 92.2 us -> none  [the longest x1 80.7 us: per_device(): tangent = project(shard_piece.reshape(shard_piece.shape[0], probe_width))]
    all_to_all x0 -> x1, blocking collectives: none -> 51.6 us  [gather_tokens(): result = lax.all_to_all(result, 'dp', 0, 0, tiled=True)]
    unnamed x2 -> x35, local copies, waits for them, and re-layouts: 0.01 us -> 25.7 us
    dot_general x4 -> x9, matrix products: 80.2 us -> 95.3 us  [the longest x3 35.6 us: gather_tokens(): lax.dot_general(gathered, second, (((0,), (0,)), ((), ())), preferred_ele...]
    unnamed x0 -> x14, other arithmetic: none -> 13.7 us
  transfers between devices with their start and end apart: 5 -> 7, of which waited for: 5 -> 6; matrix products, arithmetic and copies ran while one was open for 4% -> 23% of each run, Pallas kernels for 0% -> 0%
where the time goes in v1:
time: 511 us; the launch traced here: 506 us
  waiting for transfers between devices  251 us (49%)
  matrix products  95.3 us (19%)
  local copies, waits for them, and re-layouts  55.6 us (11%)
  blocking collectives  51.6 us (10%)
  other arithmetic  25.2 us (5%)
  between operations  13.6 us (3%)
  starting transfers between devices  13.4 us (3%)
    all_to_all x3, waiting for transfers between devices, swap(): return lax.all_to_all(jnp.stack(blocks), 'dp', 0, 0, tiled=True)  139 us
    all_gather x1, waiting for transfers between devices, gather_tokens(): lax.all_gather(normalize(tokens, norm_gain), 'tensor', axis=0, tiled=True)  83.6 us
    all_to_all x1, blocking collectives, gather_tokens(): result = lax.all_to_all(result, 'dp', 0, 0, tiled=True)  51.6 us
    dot_general x3, matrix products, gather_tokens(): lax.dot_general(gathered, second, (((0,), (0,)), ((), ())), preferred_ele...  35.6 us
    dot_general x3, matrix products, gather_tokens(): pre = jnp.dot(gathered, pair, preferred_element_type=jnp.float32)  31.2 us
    dot_general x3, matrix products, gather_tokens(): tangent = jnp.dot(gathered, directions, preferred_element_type=jnp.float32)  28.5 us
    all_gather x3, waiting for transfers between devices, gather_tokens(): gathered = lax.all_gather(own[start:stop], 'dp', axis=0, tiled=True)  27.8 us
    unnamed x35, local copies, waits for them, and re-layouts  25.7 us
  transfers between devices with their start and end apart: 7, of which 6 were waited for; matrix products, arithmetic and copies ran while one was open for 23% of the time, Pallas kernels for 0%

profile of v1, /device:TPU:0, one launch (start us, length us, event | category | flops | bytes accessed | tf_op | source)
XLA Modules:
  0.0 505.7 jit_solution(17145049212304228981)
XLA Ops:
  6.5 1.5 fusion
  8.1 2.5 fusion.2
  10.7 83.6 %all-gather.5.cloned.1.call-done = bf16[512,4096]{1,0:T(8,128)(2,1)} async-done(((bf16[128,4096]{1,0:T(8,128)(2,1)}), bf16[512,4096]{1,0:T(8,128)(2,1)}) %all-gather.5.cloned.1.call-update) | async-done | bytes 4194320 | tf_op jit(solution)/shard_map/all_gather | solution.py:66
  94.2 3.9 fusion.54
  104.8 3.7 all-to-all-start
  108.5 2.5 fusion.56
  111.0 0.8 fusion.31
  113.4 0.9 fusion.34
  114.3 0.8 fusion.35
  115.2 0.8 fusion.36
  116.0 0.8 fusion.37
  116.8 0.9 fusion.38
  117.7 30.4 %all-to-all-done = bf16[8,512,256]{2,1,0:T(8,128)(2,1)S(1)} async-done(((bf16[8,512,256]{2,1,0:T(8,128)(2,1)}), bf16[8,512,256]{2,1,0:T(8,128)(2,1)S(1)}, u32[]{:S(2)}, u32[]{:S(2)}) %all-to-all-start) | async-done | bytes 2097184 | tf_op jit(solution)/shard_map/all_to_all | solution.py:61
  148.1 4.6 all-to-all-start.1
  152.7 5.8 %copy.14 = bf16[64,8,2,2048]{3,1,2,0:T(8,128)(2,1)S(1)} copy(bf16[64,8,2,2048]{3,2,1,0:T(2,128)(2,1)} %bitcast.126) | data formatting | bytes 8388608
  158.6 1.2 fusion.53
  159.8 0.8 fusion.39
  160.6 0.8 fusion.40
  161.4 0.8 fusion.41
  162.3 0.8 fusion.42
  163.1 2.3 slice.336
  165.4 1.9 fusion.43
  167.3 1.8 fusion.44
  169.1 0.8 fusion.45
  169.9 0.8 fusion.46
  170.7 64.2 %all-to-all-done.1 = bf16[8,512,512]{2,1,0:T(8,128)(2,1)} async-done(((bf16[8,512,512]{2,1,0:T(8,128)(2,1)}), bf16[8,512,512]{2,1,0:T(8,128)(2,1)}, u32[]{:S(2)}, u32[]{:S(2)}) %all-to-all-start.1) | async-done | bytes 4194336 | tf_op jit(solution)/shard_map/all_to_all | solution.py:61
  235.0 5.1 %all-to-all-start.2 = ((bf16[8,512,512]{2,1,0:T(8,128)(2,1)}), bf16[8,512,512]{2,1,0:T(8,128)(2,1)}, u32[]{:S(2)}, u32[]{:S(2)}) async-start(bf16[8,512,512]{2,1,0:T(8,128)(2,1)} %fusion.46), calls=%async_computation.2 | async-start | bytes 8388608 | tf_op jit(solution)/shard_map/all_to_all | solution.py:61
  240.2 1.3 bitcast_convert_fusion.1
  241.5 3.0 copy.10
  244.5 1.3 bitcast_convert_fusion
  245.8 3.3 copy.11
  249.5 12.2 %fusion.58 = f32[1536,512]{0,1:T(8,128)} fusion(bf16[1536,4096]{1,0:T(8,128)(2,1)} %all-gather.11.cloned.1.call-done, bf16[4096,512]{1,0:T(8,128)(2,1)} %bitcast.17), kind=kOutput, calls=%fused_computation.120 | convolution fusion | flops 6442450944 | bytes 19922944 | tf_op jit(solution)/shard_map/dot_general | solution.py:90
  261.7 44.2 %all-to-all-done.2 = bf16[8,512,512]{2,1,0:T(8,128)(2,1)} async-done(((bf16[8,512,512]{2,1,0:T(8,128)(2,1)}), bf16[8,512,512]{2,1,0:T(8,128)(2,1)}, u32[]{:S(2)}, u32[]{:S(2)}) %all-to-all-start.2) | async-done | bytes 4194336 | tf_op jit(solution)/shard_map/all_to_all | solution.py:61
  306.0 11.1 %fusion.59 = f32[1536,512]{0,1:T(8,128)S(1)} fusion(bf16[1536,4096]{1,0:T(8,128)(2,1)} %all-gather.11.cloned.1.call-done, bf16[4096,512]{1,0:T(8,128)(2,1)} %bitcast.26), kind=kOutput, calls=%fused_computation.121 | convolution fusion | flops 6442450944 | bytes 19922944 | tf_op jit(solution)/shard_map/dot_general | solution.py:91
  317.1 0.9 fusion.14
  318.3 3.5 copy-done.4
  321.8 10.7 %fusion.15 = f32[4096,512]{1,0:T(8,128)} fusion(bf16[1536,4096]{1,0:T(8,128)(2,1)S(1)} %copy-done.4, bf16[1536,256]{0,1:T(8,128)(2,1)S(1)} %fusion.13, bf16[1536,256]{0,1:T(8,128)(2,1)S(1)} %get-tuple-element.17), kind=kOutput, calls=%fused_computation.25 | convolution fusion | flops 6445596672 | bytes 22544384 | tf_op jit(solution)/shard_map/dot_general | solution.py:101
  332.5 10.7 %all-gather.9.cloned.1.call-done = bf16[1536,4096]{1,0:T(8,128)(2,1)} async-done(((bf16[192,4096]{1,0:T(8,128)(2,1)}), bf16[1536,4096]{1,0:T(8,128)(2,1)}) %all-gather.9.cloned.1.call-update) | async-done | bytes 12582928 | tf_op jit(solution)/shard_map/all_gather | solution.py:87
  343.2 10.6 %fusion.60 = f32[1536,512]{0,1:T(8,128)S(1)} fusion(bf16[1536,4096]{1,0:T(8,128)(2,1)} %all-gather.9.cloned.1.call-done, bf16[4096,512]{1,0:T(8,128)(2,1)} %bitcast.17), kind=kOutput, calls=%fused_computation.122 | convolution fusion | flops 6442450944 | bytes 19922944 | tf_op jit(solution)/shard_map/dot_general | solution.py:90
  353.8 10.8 %fusion.61 = f32[1536,512]{0,1:T(8,128)S(1)} fusion(bf16[1536,4096]{1,0:T(8,128)(2,1)} %all-gather.9.cloned.1.call-done, bf16[4096,512]{1,0:T(8,128)(2,1)} %bitcast.26), kind=kOutput, calls=%fused_computation.123 | convolution fusion | flops 6442450944 | bytes 19922944 | tf_op jit(solution)/shard_map/dot_general | solution.py:91
  364.7 0.9 fusion.12
  365.8 16.2 %convolution_add_fusion = f32[4096,512]{1,0:T(8,128)} fusion(f32[4096,512]{1,0:T(8,128)} %fusion.15, bf16[1536,4096]{1,0:T(8,128)(2,1)} %all-gather.9.cloned.1.call-done, bf16[1536,256]{0,1:T(8,128)(2,1)S(1)} %fusion.11, bf16[1536,256]{0,1:T(8,128)(2,1)S(1)} %get-tuple-element.15), kind=kOutput, calls=%fused_computation.1 | convolution fusion | flops 6447693824 | bytes 30932992 | tf_op jit(solution)/shard_map/dot_general | solution.py:101
  382.1 17.1 %all-gather.7.cloned.1.call-done = bf16[1024,4096]{1,0:T(8,128)(2,1)} async-done(((bf16[128,4096]{1,0:T(8,128)(2,1)}), bf16[1024,4096]{1,0:T(8,128)(2,1)}) %all-gather.7.cloned.1.call-update) | async-done | bytes 8388624 | tf_op jit(solution)/shard_map/all_gather | solution.py:87
  399.2 8.4 %fusion.62 = f32[1024,512]{0,1:T(8,128)S(1)} fusion(bf16[1024,4096]{1,0:T(8,128)(2,1)} %all-gather.7.cloned.1.call-done, bf16[4096,512]{1,0:T(8,128)(2,1)} %bitcast.17), kind=kOutput, calls=%fused_computation.124 | convolution fusion | flops 4294967296 | bytes 14680064 | tf_op jit(solution)/shard_map/dot_general | solution.py:90
  407.6 6.5 %fusion.63 = f32[1024,512]{0,1:T(8,128)S(1)} fusion(bf16[1024,4096]{1,0:T(8,128)(2,1)S(1)} %copy-done.5, bf16[4096,512]{1,0:T(8,128)(2,1)} %bitcast.26), kind=kOutput, calls=%fused_computation.125 | convolution fusion | flops 4294967296 | bytes 14680064 | tf_op jit(solution)/shard_map/dot_general | solution.py:91
  414.9 8.7 %add_convert_fusion = bf16[4096,512]{1,0:T(8,128)(2,1)S(1)} fusion(f32[4096,512]{1,0:T(8,128)} %convolution_add_fusion, bf16[1024,4096]{1,0:T(8,128)(2,1)S(1)} %copy-done.5, bf16[1024,256]{0,1:T(8,128)(2,1)S(1)} %fusion.26, bf16[1024,256]{0,1:T(8,128)(2,1)S(1)} %get-tuple-element.13), kind=kOutput, calls=%fused_computation | convolution fusion | flops 4301258752 | bytes 22020096 | tf_op jit(solution)/shard_map/dot_general | solution.py:101
  423.5 51.6 %all_to_all.20 = bf16[8,512,512]{2,1,0:T(8,128)(2,1)S(1)} all-to-all(bf16[8,512,512]{2,1,0:T(8,128)(2,1)S(1)} %bitcast.127), channel_id=1, replica_groups=mesh['dp'=8,'tensor'=4] {'dp'}, dimensions={0} | all-to-all | bytes 8388608 | tf_op jit(solution)/shard_map/all_to_all | solution.py:108
  487.4 11.5 %reshape.40 = f32[512,2,2048]{2,1,0:T(2,128)} reshape(bf16[512,4096]{1,0:T(8,128)(2,1)} %slice_dynamic-update-slice_fusion) | data formatting | bytes 12582912 | tf_op jit(solution)/shard_map/convert_element_type | solution.py:112
  (56 shorter events, 22.6 us)
Async XLA Ops:
  6.5 87.7 %all-gather.5.cloned.1.call-start = ((), (), s32[]{:S(2)}) async-start(), calls=%async_computation.4 | async-start | bytes 5242880 | tf_op jit(solution)/shard_map/all_gather | solution.py:66
  10.6 88.3 %copy-start.3 = (bf16[512,2048]{1,0:T(8,128)(2,1)S(1)}, bf16[512,2048]{1,0:T(8,128)(2,1)}, u32[]{:S(2)}) copy-start(bf16[512,2048]{1,0:T(8,128)(2,1)} %param.11) | copy-start | bytes 6291460
  10.6 238.9 %all-gather.11.cloned.1.call-start = ((), (), s32[]{:S(2)}) async-start(), calls=%async_computation.7 | async-start | bytes 14155776 | tf_op jit(solution)/shard_map/all_gather | solution.py:87
  98.1 245.0 %all-gather.9.cloned.1.call-start = ((), (), s32[]{:S(2)}) async-start(), calls=%async_computation.6 | async-start | bytes 14155776 | tf_op jit(solution)/shard_map/all_gather | solution.py:87
  104.8 43.3 %all-to-all-start = ((bf16[8,512,256]{2,1,0:T(8,128)(2,1)}), bf16[8,512,256]{2,1,0:T(8,128)(2,1)S(1)}, u32[]{:S(2)}, u32[]{:S(2)}) async-start(bf16[8,512,256]{2,1,0:T(8,128)(2,1)} %bitcast_dynamic-update-slice_fusion), calls=%async_computation | async-start | bytes 4194304 | tf_op jit(solution)/shard_map/all_to_all | solution.py:61
  148.1 86.9 %all-to-all-start.1 = ((bf16[8,512,512]{2,1,0:T(8,128)(2,1)}), bf16[8,512,512]{2,1,0:T(8,128)(2,1)}, u32[]{:S(2)}, u32[]{:S(2)}) async-start(bf16[8,512,512]{2,1,0:T(8,128)(2,1)} %fusion.38), calls=%async_computation.1 | async-start | bytes 8388608 | tf_op jit(solution)/shard_map/all_to_all | solution.py:61
  152.7 246.5 %all-gather.7.cloned.1.call-start = ((), (), s32[]{:S(2)}) async-start(), calls=%async_computation.5 | async-start | bytes 9437184 | tf_op jit(solution)/shard_map/all_gather | solution.py:87
  235.0 71.0 %all-to-all-start.2 = ((bf16[8,512,512]{2,1,0:T(8,128)(2,1)}), bf16[8,512,512]{2,1,0:T(8,128)(2,1)}, u32[]{:S(2)}, u32[]{:S(2)}) async-start(bf16[8,512,512]{2,1,0:T(8,128)(2,1)} %fusion.46), calls=%async_computation.2 | async-start | bytes 8388608 | tf_op jit(solution)/shard_map/all_to_all | solution.py:61
  306.0 11.2 %copy-start.1 = (f32[1536,256]{0,1:T(8,128)S(1)}, f32[1536,256]{0,1:T(8,128)}, u32[]{:S(2)}) copy-start(f32[1536,256]{0,1:T(8,128)} %copy.10) | copy-start | bytes 4718596
  306.0 11.2 %copy-start.2 = (f32[1536,512]{0,1:T(8,128)S(1)}, f32[1536,512]{0,1:T(8,128)}, u32[]{:S(2)}) copy-start(f32[1536,512]{0,1:T(8,128)} %fusion.58) | copy-start | bytes 9437188
  317.1 4.6 copy-start.4
  353.8 10.9 %copy-start = (f32[1536,256]{0,1:T(8,128)S(1)}, f32[1536,256]{0,1:T(8,128)}, u32[]{:S(2)}) copy-start(f32[1536,256]{0,1:T(8,128)} %copy.11) | copy-start | bytes 4718596
  399.2 8.4 %copy-start.5 = (bf16[1024,4096]{1,0:T(8,128)(2,1)S(1)}, bf16[1024,4096]{1,0:T(8,128)(2,1)}, u32[]{:S(2)}) copy-start(bf16[1024,4096]{1,0:T(8,128)(2,1)} %all-gather.7.cloned.1.call-done) | copy-start | bytes 25165828
Sparse Core Ops, SparseCore 0:
  10.7 83.4 all-gather.4
  98.3 126.6 all-gather.10
  226.9 116.2 all-gather.8
  344.9 54.2 all-gather.6

commit v2 on v1

--- a/solution.py
+++ b/solution.py
@@ -3,6 +3,7 @@
 import jax
 import jax.numpy as jnp
 from jax import lax
+from jax.experimental import pallas as pl
 from jax.sharding import PartitionSpec as P
 
 LANES = 128
@@ -50,6 +51,27 @@
     return result.reshape(local_depth, probe_count, local_units)
 
 
+def unpack(blocks, probe_count):
+    ways, local_depth, width = blocks.shape
+    units = width // probe_count
+    rows = math.gcd(local_depth, 64)
+
+    def kernel(blocks_ref, out_ref):
+        for p in range(probe_count):
+            for j in range(ways):
+                piece = blocks_ref[j, :, p * units : (p + 1) * units]
+                out_ref[:, p, j * units : (j + 1) * units] = piece.astype(jnp.float32)
+
+    return pl.pallas_call(
+        kernel,
+        grid=(local_depth // rows,),
+        in_specs=[pl.BlockSpec((ways, rows, width), lambda i: (0, i, 0))],
+        out_specs=pl.BlockSpec((rows, probe_count, ways * units), lambda i: (i, 0, 0)),
+        out_shape=jax.ShapeDtypeStruct((local_depth, probe_count, ways * units), jnp.float32),
+        name="unpack",
+    )(blocks)
+
+
 def gather_tokens(tokens, norm_gain, w_gate, w_up, probes, cotangent):
     ways = lax.axis_size("dp")
     local_depth, probe_count, local_units = probes.shape
@@ -79,6 +101,8 @@
         ]
     ).reshape(depth, probe_count * units)
 
+    own, pair, cot = lax.optimization_barrier((own, pair, cot))
+
     scale_factor = 1.0 / math.sqrt(group * ways)
     total = None
     start = 0
@@ -106,10 +130,7 @@
 
     result = total.astype(jnp.bfloat16).reshape(ways, local_depth, probe_count * units)
     result = lax.all_to_all(result, "dp", 0, 0, tiled=True)
-    flat = jnp.concatenate(
-        [columns(result[j], p) for p in range(probe_count) for j in range(ways)], axis=1
-    )
-    return flat.reshape(local_depth, probe_count, local_units).astype(jnp.float32)
+    return unpack(result, probe_count)
 
 
 def per_device(tokens, norm_gain, w_gate, w_up, probes, cotangent):

time: 511 us -> 443 us (0.87)
  waiting for transfers between devices: 251 us -> 152 us
  blocking collectives: 51.6 us -> 106 us
  local copies, waits for them, and re-layouts: 55.6 us -> 27.9 us
  Pallas kernels: 0 us -> 9.1 us
    all_to_all x3 -> x2, waiting for transfers between devices: 139 us -> 17.1 us  [swap(): return lax.all_to_all(jnp.stack(blocks), 'dp', 0, 0, tiled=True)]
    all_gather x3, waiting for transfers between devices: 27.8 us -> 135 us  [gather_tokens(): gathered = lax.all_gather(own[start:stop], 'dp', axis=0, tiled=True)]
    all_gather x1, waiting for transfers between devices: 83.6 us -> 0.01 us  [gather_tokens(): lax.all_gather(normalize(tokens, norm_gain), 'tensor', axis=0, tiled=True)]
    all_to_all x0 -> x1, blocking collectives: none -> 53.5 us  [swap(): return lax.all_to_all(jnp.stack(blocks), 'dp', 0, 0, tiled=True)]
    unnamed x35 -> x22, local copies, waits for them, and re-layouts: 25.7 us -> 13.2 us
    convert_element_type x1 -> x0, local copies, waits for them, and re-layouts: 11.5 us -> none  [gather_tokens(): flat.reshape(local_depth, probe_count, local_units).astype(jnp.float32)]
    pallas_call x0 -> x1, Pallas kernels: none -> 9.1 us  [unpack(): pl.pallas_call(kernel, grid=(local_depth // rows,), in_specs=[pl.BlockSpe...]
    all_to_all x3 -> x2, starting transfers between devices: 13.3 us -> 10.3 us  [swap(): return lax.all_to_all(jnp.stack(blocks), 'dp', 0, 0, tiled=True)]
  transfers between devices with their start and end apart: 7 -> 6, of which waited for: 6 -> 4; matrix products, arithmetic and copies ran while one was open for 23% -> 25% of each run, Pallas kernels for 0% -> 0%
where the time goes in v2:
time: 443 us; the launch traced here: 437 us
  waiting for transfers between devices  152 us (34%)
  blocking collectives  106 us (24%)
  matrix products  95.2 us (21%)
  local copies, waits for them, and re-layouts  27.9 us (6%)
  other arithmetic  23 us (5%)
  between operations  13.6 us (3%)
  starting transfers between devices  10.4 us (2%)
  Pallas kernels  9.1 us (2%)
    all_gather x3, waiting for transfers between devices, gather_tokens(): gathered = lax.all_gather(own[start:stop], 'dp', axis=0, tiled=True)  135 us
    all_to_all x1, blocking collectives, swap(): return lax.all_to_all(jnp.stack(blocks), 'dp', 0, 0, tiled=True)  53.5 us
    all_to_all x1, blocking collectives, gather_tokens(): result = lax.all_to_all(result, 'dp', 0, 0, tiled=True)  52.3 us
    dot_general x3, matrix products, gather_tokens(): lax.dot_general(gathered, second, (((0,), (0,)), ((), ())), preferred_ele...  35.9 us
    dot_general x3, matrix products, gather_tokens(): pre = jnp.dot(gathered, pair, preferred_element_type=jnp.float32)  31.2 us
    dot_general x3, matrix products, gather_tokens(): tangent = jnp.dot(gathered, directions, preferred_element_type=jnp.float32)  28.1 us
    all_to_all x2, waiting for transfers between devices, swap(): return lax.all_to_all(jnp.stack(blocks), 'dp', 0, 0, tiled=True)  17.1 us
    unnamed x14, other arithmetic  13.6 us
  transfers between devices with their start and end apart: 6, of which 4 were waited for; matrix products, arithmetic and copies ran while one was open for 25% of the time, Pallas kernels for 0%

profile of v2, /device:TPU:0, one launch (start us, length us, event | category | flops | bytes accessed | tf_op | source)
XLA Modules:
  0.0 437.4 jit_solution(13370281724385577872)
XLA Ops:
  6.5 1.7 fusion
  8.2 2.6 fusion.2
  13.0 0.8 bitcast_dynamic-update-slice_fusion.4
  15.3 0.8 bitcast_dynamic-update-slice_fusion.1
  16.8 5.2 %all-to-all-start.1 = ((bf16[8,512,256]{2,1,0:T(8,128)(2,1)}), bf16[8,512,256]{2,1,0:T(8,128)(2,1)S(1)}, u32[]{:S(2)}, u32[]{:S(2)}) async-start(bf16[8,512,256]{2,1,0:T(8,128)(2,1)} %bitcast_dynamic-update-slice_fusion), calls=%async_computation.1 | async-start | bytes 4194304 | tf_op jit(solution)/shard_map/all_to_all | solution.py:83
  22.0 2.8 fusion.56
  24.8 0.8 fusion.31
  25.6 0.8 fusion.32
  26.5 0.8 fusion.33
  27.3 0.8 fusion.34
  28.1 0.8 fusion.35
  29.0 0.8 fusion.36
  29.8 0.8 fusion.37
  30.6 0.8 fusion.38
  31.5 17.1 %all-to-all-done.1 = bf16[8,512,256]{2,1,0:T(8,128)(2,1)S(1)} async-done(((bf16[8,512,256]{2,1,0:T(8,128)(2,1)}), bf16[8,512,256]{2,1,0:T(8,128)(2,1)S(1)}, u32[]{:S(2)}, u32[]{:S(2)}) %all-to-all-start.1) | async-done | bytes 2097184 | tf_op jit(solution)/shard_map/all_to_all | solution.py:83
  48.6 53.5 %all_to_all.20 = bf16[8,512,512]{2,1,0:T(8,128)(2,1)} all-to-all(bf16[8,512,512]{2,1,0:T(8,128)(2,1)} %fusion.38), channel_id=1, replica_groups=mesh['dp'=8,'tensor'=4] {'dp'}, dimensions={0} | all-to-all | bytes 8388608 | tf_op jit(solution)/shard_map/all_to_all | solution.py:83
  102.1 3.9 fusion.54
  106.8 4.6 %copy.14 = bf16[64,8,2,2048]{3,1,2,0:T(8,128)(2,1)S(1)} copy(bf16[64,8,2,2048]{3,2,1,0:T(2,128)(2,1)} %bitcast.110) | data formatting | bytes 8388608
  111.4 1.2 fusion.53
  112.6 0.8 fusion.39
  113.4 0.8 fusion.40
  114.3 0.8 fusion.41
  115.1 0.8 fusion.42
  115.9 2.3 slice.198
  118.3 1.9 fusion.43
  120.1 1.8 fusion.44
  121.9 0.8 fusion.45
  122.7 0.8 fusion.46
  123.6 5.1 %all-to-all-start.2 = ((bf16[8,512,512]{2,1,0:T(8,128)(2,1)}), bf16[8,512,512]{2,1,0:T(8,128)(2,1)}, u32[]{:S(2)}, u32[]{:S(2)}) async-start(bf16[8,512,512]{2,1,0:T(8,128)(2,1)} %fusion.46), calls=%async_computation.2 | async-start | bytes 8388608 | tf_op jit(solution)/shard_map/all_to_all | solution.py:83
  129.0 1.6 copy.10
  130.8 1.6 copy.11
  132.8 82.1 %all-gather.11.cloned.1.call-done = bf16[1536,4096]{1,0:T(8,128)(2,1)} async-done(((bf16[192,4096]{1,0:T(8,128)(2,1)}), bf16[1536,4096]{1,0:T(8,128)(2,1)}) %all-gather.11.cloned.1.call-update) | async-done | bytes 12582928 | tf_op jit(solution)/shard_map/all_gather | solution.py:111
  214.9 12.2 %fusion.58 = f32[1536,512]{0,1:T(8,128)} fusion(bf16[1536,4096]{1,0:T(8,128)(2,1)} %all-gather.11.cloned.1.call-done, bf16[4096,512]{1,0:T(8,128)(2,1)} %bitcast.111), kind=kOutput, calls=%fused_computation.96 | convolution fusion | flops 6442450944 | bytes 19922944 | tf_op jit(solution)/shard_map/dot_general | solution.py:114
  227.1 10.8 %fusion.59 = f32[1536,512]{0,1:T(8,128)S(1)} fusion(bf16[1536,4096]{1,0:T(8,128)(2,1)} %all-gather.11.cloned.1.call-done, bf16[4096,512]{1,0:T(8,128)(2,1)} %bitcast.26), kind=kOutput, calls=%fused_computation.97 | convolution fusion | flops 6442450944 | bytes 19922944 | tf_op jit(solution)/shard_map/dot_general | solution.py:115
  237.9 0.9 fusion.14
  239.1 3.4 copy-done.5
  242.5 11.0 %fusion.15 = f32[4096,512]{1,0:T(8,128)} fusion(bf16[1536,4096]{1,0:T(8,128)(2,1)S(1)} %copy-done.5, bf16[1536,256]{0,1:T(8,128)(2,1)S(1)} %fusion.13, bf16[1536,256]{0,1:T(8,128)(2,1)S(1)} %get-tuple-element.23), kind=kOutput, calls=%fused_computation.25 | convolution fusion | flops 6445596672 | bytes 22544384 | tf_op jit(solution)/shard_map/dot_general | solution.py:125
  253.5 35.3 %all-gather.9.cloned.1.call-done = bf16[1536,4096]{1,0:T(8,128)(2,1)} async-done(((bf16[192,4096]{1,0:T(8,128)(2,1)}), bf16[1536,4096]{1,0:T(8,128)(2,1)}) %all-gather.9.cloned.1.call-update) | async-done | bytes 12582928 | tf_op jit(solution)/shard_map/all_gather | solution.py:111
  288.8 10.6 %fusion.60 = f32[1536,512]{0,1:T(8,128)S(1)} fusion(bf16[1536,4096]{1,0:T(8,128)(2,1)} %all-gather.9.cloned.1.call-done, bf16[4096,512]{1,0:T(8,128)(2,1)} %bitcast.112), kind=kOutput, calls=%fused_computation.98 | convolution fusion | flops 6442450944 | bytes 19922944 | tf_op jit(solution)/shard_map/dot_general | solution.py:114
  299.5 10.8 %fusion.61 = f32[1536,512]{0,1:T(8,128)S(1)} fusion(bf16[1536,4096]{1,0:T(8,128)(2,1)} %all-gather.9.cloned.1.call-done, bf16[4096,512]{1,0:T(8,128)(2,1)} %bitcast.26), kind=kOutput, calls=%fused_computation.99 | convolution fusion | flops 6442450944 | bytes 19922944 | tf_op jit(solution)/shard_map/dot_general | solution.py:115
  310.3 0.9 fusion.12
  311.5 16.2 %convolution_add_fusion = f32[4096,512]{1,0:T(8,128)} fusion(f32[4096,512]{1,0:T(8,128)} %fusion.15, bf16[1536,4096]{1,0:T(8,128)(2,1)} %all-gather.9.cloned.1.call-done, bf16[1536,256]{0,1:T(8,128)(2,1)S(1)} %fusion.11, bf16[1536,256]{0,1:T(8,128)(2,1)S(1)} %get-tuple-element.21), kind=kOutput, calls=%fused_computation.1 | convolution fusion | flops 6447693824 | bytes 30932992 | tf_op jit(solution)/shard_map/dot_general | solution.py:125
  327.7 17.1 %all-gather.7.cloned.1.call-done = bf16[1024,4096]{1,0:T(8,128)(2,1)} async-done(((bf16[128,4096]{1,0:T(8,128)(2,1)}), bf16[1024,4096]{1,0:T(8,128)(2,1)}) %all-gather.7.cloned.1.call-update) | async-done | bytes 8388624 | tf_op jit(solution)/shard_map/all_gather | solution.py:111
  344.9 8.4 %fusion.62 = f32[1024,512]{0,1:T(8,128)S(1)} fusion(bf16[1024,4096]{1,0:T(8,128)(2,1)} %all-gather.7.cloned.1.call-done, bf16[4096,512]{1,0:T(8,128)(2,1)} %bitcast.113), kind=kOutput, calls=%fused_computation.100 | convolution fusion | flops 4294967296 | bytes 14680064 | tf_op jit(solution)/shard_map/dot_general | solution.py:114
  353.3 6.5 %fusion.63 = f32[1024,512]{0,1:T(8,128)S(1)} fusion(bf16[1024,4096]{1,0:T(8,128)(2,1)S(1)} %copy-done.6, bf16[4096,512]{1,0:T(8,128)(2,1)} %bitcast.26), kind=kOutput, calls=%fused_computation.101 | convolution fusion | flops 4294967296 | bytes 14680064 | tf_op jit(solution)/shard_map/dot_general | solution.py:115
  360.5 8.7 %add_convert_fusion = bf16[4096,512]{1,0:T(8,128)(2,1)S(1)} fusion(f32[4096,512]{1,0:T(8,128)} %convolution_add_fusion, bf16[1024,4096]{1,0:T(8,128)(2,1)S(1)} %copy-done.6, bf16[1024,256]{0,1:T(8,128)(2,1)S(1)} %fusion.26, bf16[1024,256]{0,1:T(8,128)(2,1)S(1)} %get-tuple-element.19), kind=kOutput, calls=%fused_computation | convolution fusion | flops 4301258752 | bytes 22020096 | tf_op jit(solution)/shard_map/dot_general | solution.py:125
  369.2 52.3 %all_to_all.21.blocks_ref = bf16[8,512,512]{2,1,0:T(8,128)(2,1)} all-to-all(bf16[8,512,512]{2,1,0:T(8,128)(2,1)S(1)} %bitcast.114), channel_id=1, replica_groups=mesh['dp'=8,'tensor'=4] {'dp'}, dimensions={0} | all-to-all | bytes 8388608 | tf_op jit(solution)/shard_map/all_to_all | solution.py:132
  421.5 9.1 %unpack.1 = f32[512,2,2048]{2,1,0:T(2,128)} custom-call(bf16[8,512,512]{2,1,0:T(8,128)(2,1)} %all_to_all.21.blocks_ref), custom_call_target="tpu_custom_call" | custom-call | tf_op jit(solution)/shard_map/unpack/pallas_call | solution.py:65
  (41 shorter events, 7.5 us)
Async XLA Ops:
  6.5 4.3 copy-start.4
  6.5 95.6 %all-gather.5.cloned.1.call-start = ((), (), s32[]{:S(2)}) async-start(), calls=%async_computation.4 | async-start | bytes 5242880 | tf_op jit(solution)/shard_map/all_gather | solution.py:88
  16.8 31.8 %all-to-all-start.1 = ((bf16[8,512,256]{2,1,0:T(8,128)(2,1)}), bf16[8,512,256]{2,1,0:T(8,128)(2,1)S(1)}, u32[]{:S(2)}, u32[]{:S(2)}) async-start(bf16[8,512,256]{2,1,0:T(8,128)(2,1)} %bitcast_dynamic-update-slice_fusion), calls=%async_computation.1 | async-start | bytes 4194304 | tf_op jit(solution)/shard_map/all_to_all | solution.py:83
  22.0 192.9 %all-gather.11.cloned.1.call-start = ((), (), s32[]{:S(2)}) async-start(), calls=%async_computation.7 | async-start | bytes 14155776 | tf_op jit(solution)/shard_map/all_gather | solution.py:111
  48.6 80.1 %copy-start = (bf16[8,512,256]{2,1,0:T(8,128)(2,1)}, bf16[8,512,256]{2,1,0:T(8,128)(2,1)S(1)}, u32[]{:S(2)}) copy-start(bf16[8,512,256]{2,1,0:T(8,128)(2,1)S(1)} %all-to-all-done.1) | copy-start | bytes 6291460
  106.0 182.8 %all-gather.9.cloned.1.call-start = ((), (), s32[]{:S(2)}) async-start(), calls=%async_computation.6 | async-start | bytes 14155776 | tf_op jit(solution)/shard_map/all_gather | solution.py:111
  106.8 238.1 %all-gather.7.cloned.1.call-start = ((), (), s32[]{:S(2)}) async-start(), calls=%async_computation.5 | async-start | bytes 9437184 | tf_op jit(solution)/shard_map/all_gather | solution.py:111
  123.6 103.5 %all-to-all-start.2 = ((bf16[8,512,512]{2,1,0:T(8,128)(2,1)}), bf16[8,512,512]{2,1,0:T(8,128)(2,1)}, u32[]{:S(2)}, u32[]{:S(2)}) async-start(bf16[8,512,512]{2,1,0:T(8,128)(2,1)} %fusion.46), calls=%async_computation.2 | async-start | bytes 8388608 | tf_op jit(solution)/shard_map/all_to_all | solution.py:83
  130.6 1.8 slice-start
  227.1 10.8 %copy-start.2 = (f32[1536,256]{0,1:T(8,128)S(1)}, f32[1536,256]{0,1:T(8,128)}, u32[]{:S(2)}) copy-start(f32[1536,256]{0,1:T(8,128)} %copy.10) | copy-start | bytes 4718596
  227.1 10.8 %copy-start.3 = (f32[1536,512]{0,1:T(8,128)S(1)}, f32[1536,512]{0,1:T(8,128)}, u32[]{:S(2)}) copy-start(f32[1536,512]{0,1:T(8,128)} %fusion.58) | copy-start | bytes 9437188
  237.9 4.6 %copy-start.5 = (bf16[1536,4096]{1,0:T(8,128)(2,1)S(1)}, bf16[1536,4096]{1,0:T(8,128)(2,1)}, u32[]{:S(2)}) copy-start(bf16[1536,4096]{1,0:T(8,128)(2,1)} %all-gather.11.cloned.1.call-done) | copy-start | bytes 37748740
  299.5 10.9 %copy-start.1 = (f32[1536,256]{0,1:T(8,128)S(1)}, f32[1536,256]{0,1:T(8,128)}, u32[]{:S(2)}) copy-start(f32[1536,256]{0,1:T(8,128)} %copy.11) | copy-start | bytes 4718596
  344.9 8.4 %copy-start.6 = (bf16[1024,4096]{1,0:T(8,128)(2,1)S(1)}, bf16[1024,4096]{1,0:T(8,128)(2,1)}, u32[]{:S(2)}) copy-start(bf16[1024,4096]{1,0:T(8,128)(2,1)} %all-gather.7.cloned.1.call-done) | copy-start | bytes 25165828
Sparse Core Ops, SparseCore 0:
  10.9 83.4 all-gather.4
  106.1 108.7 all-gather.10
  216.8 71.9 all-gather.8
  290.6 54.2 all-gather.6

commit v3 on v2

--- a/solution.py
+++ b/solution.py
@@ -7,7 +7,7 @@
 from jax.sharding import PartitionSpec as P
 
 LANES = 128
-PARTS = (3, 3, 2)
+PARTS = (5, 3)
 
 
 def normalize(tokens, norm_gain):

time: 443 us -> 437 us (0.986)
  matrix products: 95.2 us -> 89.7 us
  other arithmetic: 23 us -> 27.8 us
    dot_general x3 -> x2, matrix products: 35.9 us -> 32.1 us  [gather_tokens(): lax.dot_general(gathered, second, (((0,), (0,)), ((), ())), preferred_ele...]
    unnamed x22 -> x16, local copies, waits for them, and re-layouts: 13.2 us -> 10.5 us
    dot_general x3 -> x2, matrix products: 31.2 us -> 28.7 us  [gather_tokens(): pre = jnp.dot(gathered, pair, preferred_element_type=jnp.float32)]
    all_gather x3 -> x2, waiting for transfers between devices: 135 us -> 132 us  [gather_tokens(): gathered = lax.all_gather(own[start:stop], 'dp', axis=0, tiled=True)]
    dot_general x3 -> x2, matrix products: 28.1 us -> 28.9 us  [gather_tokens(): tangent = jnp.dot(gathered, directions, preferred_element_type=jnp.float32)]
  transfers between devices with their start and end apart: 6 -> 5, of which waited for: 4 -> 3; matrix products, arithmetic and copies ran while one was open for 25% -> 23% of each run, Pallas kernels for 0% -> 0%
where the time goes in v3:
time: 437 us; the launch traced here: 432 us
  waiting for transfers between devices  149 us (34%)
  blocking collectives  106 us (24%)
  matrix products  89.7 us (21%)
  other arithmetic  27.8 us (6%)
  local copies, waits for them, and re-layouts  26 us (6%)
  between operations  13.5 us (3%)
  starting transfers between devices  10.4 us (2%)
  Pallas kernels  9.1 us (2%)
    all_gather x2, waiting for transfers between devices, gather_tokens(): gathered = lax.all_gather(own[start:stop], 'dp', axis=0, tiled=True)  132 us
    all_to_all x1, blocking collectives, swap(): return lax.all_to_all(jnp.stack(blocks), 'dp', 0, 0, tiled=True)  53.5 us
    all_to_all x1, blocking collectives, gather_tokens(): result = lax.all_to_all(result, 'dp', 0, 0, tiled=True)  52.3 us
    dot_general x2, matrix products, gather_tokens(): lax.dot_general(gathered, second, (((0,), (0,)), ((), ())), preferred_ele...  32.1 us
    dot_general x2, matrix products, gather_tokens(): tangent = jnp.dot(gathered, directions, preferred_element_type=jnp.float32)  28.9 us
    dot_general x2, matrix products, gather_tokens(): pre = jnp.dot(gathered, pair, preferred_element_type=jnp.float32)  28.7 us
    all_to_all x2, waiting for transfers between devices, swap(): return lax.all_to_all(jnp.stack(blocks), 'dp', 0, 0, tiled=True)  17.1 us
    unnamed x14, other arithmetic  11.6 us
  transfers between devices with their start and end apart: 5, of which 3 were waited for; matrix products, arithmetic and copies ran while one was open for 23% of the time, Pallas kernels for 0%

profile of v3, /device:TPU:0, one launch (start us, length us, event | category | flops | bytes accessed | tf_op | source)
XLA Modules:
  0.0 431.7 jit_solution(13522099878992978573)
XLA Ops:
  6.5 1.7 fusion.10
  8.2 2.6 fusion.12
  10.8 0.7 bitcast_dynamic-update-slice_fusion.7
  12.3 0.7 bitcast_dynamic-update-slice_fusion.5
  13.8 0.8 bitcast_dynamic-update-slice_fusion.3
  14.5 0.7 bitcast_dynamic-update-slice_fusion.2
  15.3 0.7 bitcast_dynamic-update-slice_fusion.1
  16.0 0.7 bitcast_dynamic-update-slice_fusion
  16.7 5.2 %all-to-all-start.1 = ((bf16[8,512,256]{2,1,0:T(8,128)(2,1)}), bf16[8,512,256]{2,1,0:T(8,128)(2,1)S(1)}, u32[]{:S(2)}, u32[]{:S(2)}) async-start(bf16[8,512,256]{2,1,0:T(8,128)(2,1)} %bitcast_dynamic-update-slice_fusion), calls=%async_computation.1 | async-start | bytes 4194304 | tf_op jit(solution)/shard_map/all_to_all | solution.py:83
  22.0 2.8 fusion.43
  24.8 0.8 fusion.22
  25.6 0.8 fusion.23
  26.5 0.8 fusion.24
  27.3 0.8 fusion.25
  28.1 0.8 fusion.26
  28.9 0.8 fusion.27
  29.8 0.8 fusion.28
  30.6 0.8 fusion.29
  31.4 17.1 %all-to-all-done.1 = bf16[8,512,256]{2,1,0:T(8,128)(2,1)S(1)} async-done(((bf16[8,512,256]{2,1,0:T(8,128)(2,1)}), bf16[8,512,256]{2,1,0:T(8,128)(2,1)S(1)}, u32[]{:S(2)}, u32[]{:S(2)}) %all-to-all-start.1) | async-done | bytes 2097184 | tf_op jit(solution)/shard_map/all_to_all | solution.py:83
  48.6 53.5 %all_to_all.20 = bf16[8,512,512]{2,1,0:T(8,128)(2,1)} all-to-all(bf16[8,512,512]{2,1,0:T(8,128)(2,1)} %fusion.29), channel_id=1, replica_groups=mesh['dp'=8,'tensor'=4] {'dp'}, dimensions={0} | all-to-all | bytes 8388608 | tf_op jit(solution)/shard_map/all_to_all | solution.py:83
  102.1 3.5 slice.181
  105.7 2.7 slice.180
  108.4 4.6 %copy.11 = bf16[64,8,2,2048]{3,1,2,0:T(8,128)(2,1)S(1)} copy(bf16[64,8,2,2048]{3,2,1,0:T(2,128)(2,1)} %bitcast.102) | data formatting | bytes 8388608
  113.4 0.8 fusion.30
  114.3 0.8 fusion.31
  115.1 0.8 fusion.32
  115.9 0.8 fusion.33
  116.8 0.8 fusion.34
  117.6 0.8 fusion.35
  118.4 0.8 fusion.36
  119.3 0.8 fusion.37
  120.1 5.1 %all-to-all-start.2 = ((bf16[8,512,512]{2,1,0:T(8,128)(2,1)}), bf16[8,512,512]{2,1,0:T(8,128)(2,1)}, u32[]{:S(2)}, u32[]{:S(2)}) async-start(bf16[8,512,512]{2,1,0:T(8,128)(2,1)} %fusion.37), calls=%async_computation.2 | async-start | bytes 8388608 | tf_op jit(solution)/shard_map/all_to_all | solution.py:83
  125.3 1.8 bitcast_convert_fusion
  127.1 2.2 copy.9
  129.3 1.4 bitcast_convert_fusion.1
  130.7 3.0 copy.10
  133.7 118.9 %all-gather.8.cloned.1.call-done = bf16[2560,4096]{1,0:T(8,128)(2,1)} async-done(((bf16[320,4096]{1,0:T(8,128)(2,1)}), bf16[2560,4096]{1,0:T(8,128)(2,1)}) %all-gather.8.cloned.1.call-update) | async-done | bytes 20971536 | tf_op jit(solution)/shard_map/all_gather | solution.py:111
  252.7 18.0 %fusion.45 = f32[2560,512]{0,1:T(8,128)} fusion(bf16[2560,4096]{1,0:T(8,128)(2,1)} %all-gather.8.cloned.1.call-done, bf16[4096,512]{1,0:T(8,128)(2,1)} %bitcast.103), kind=kOutput, calls=%fused_computation.79 | convolution fusion | flops 10737418240 | bytes 30408704 | tf_op jit(solution)/shard_map/dot_general | solution.py:114
  270.7 18.2 %fusion.46 = f32[2560,512]{0,1:T(8,128)} fusion(bf16[2560,4096]{1,0:T(8,128)(2,1)} %all-gather.8.cloned.1.call-done, bf16[4096,512]{1,0:T(8,128)(2,1)} %bitcast.26), kind=kOutput, calls=%fused_computation.80 | convolution fusion | flops 10737418240 | bytes 30408704 | tf_op jit(solution)/shard_map/dot_general | solution.py:115
  288.9 5.5 %fusion.5 = (bf16[2560,256]{0,1:T(8,128)(2,1)S(1)}, f32[2560,256]{0,1:T(8,128)S(1)}) fusion(f32[2560,512]{0,1:T(8,128)} %fusion.46, f32[2560,512]{0,1:T(8,128)} %fusion.45, f32[2560,256]{0,1:T(8,128)S(1)} %copy.9), kind=kLoop, calls=%fused_computation.11 | loop fusion | flops 9830400 | bytes 14417920 | tf_op jit(solution)/shard_map/convert_element_type | solution.py:120
  295.6 17.7 %fusion.6 = f32[4096,512]{1,0:T(8,128)} fusion(bf16[2560,4096]{1,0:T(8,128)(2,1)} %all-gather.8.cloned.1.call-done, bf16[2560,256]{0,1:T(8,128)(2,1)S(1)} %fusion.4, bf16[2560,256]{0,1:T(8,128)(2,1)S(1)} %get-tuple-element.17), kind=kOutput, calls=%fused_computation.12 | convolution fusion | flops 10742661120 | bytes 31981568 | tf_op jit(solution)/shard_map/dot_general | solution.py:125
  313.3 13.3 %all-gather.6.cloned.1.call-done = bf16[1536,4096]{1,0:T(8,128)(2,1)} async-done(((bf16[192,4096]{1,0:T(8,128)(2,1)}), bf16[1536,4096]{1,0:T(8,128)(2,1)}) %all-gather.6.cloned.1.call-update) | async-done | bytes 12582928 | tf_op jit(solution)/shard_map/all_gather | solution.py:111
  326.6 10.6 %fusion.47 = f32[1536,512]{0,1:T(8,128)S(1)} fusion(bf16[1536,4096]{1,0:T(8,128)(2,1)} %all-gather.6.cloned.1.call-done, bf16[4096,512]{1,0:T(8,128)(2,1)} %bitcast.104), kind=kOutput, calls=%fused_computation.81 | convolution fusion | flops 6442450944 | bytes 19922944 | tf_op jit(solution)/shard_map/dot_general | solution.py:114
  337.2 10.7 %fusion.48 = f32[1536,512]{0,1:T(8,128)S(1)} fusion(bf16[1536,4096]{1,0:T(8,128)(2,1)} %all-gather.6.cloned.1.call-done, bf16[4096,512]{1,0:T(8,128)(2,1)} %bitcast.26), kind=kOutput, calls=%fused_computation.82 | convolution fusion | flops 6442450944 | bytes 19922944 | tf_op jit(solution)/shard_map/dot_general | solution.py:115
  348.0 0.9 fusion.18
  349.1 14.4 %add_convert_fusion = bf16[4096,512]{1,0:T(8,128)(2,1)S(1)} fusion(f32[4096,512]{1,0:T(8,128)} %fusion.6, bf16[1536,4096]{1,0:T(8,128)(2,1)} %all-gather.6.cloned.1.call-done, bf16[1536,256]{0,1:T(8,128)(2,1)S(1)} %fusion.17, bf16[1536,256]{0,1:T(8,128)(2,1)S(1)} %get-tuple-element.15), kind=kOutput, calls=%fused_computation | convolution fusion | flops 6449790976 | bytes 26738688 | tf_op jit(solution)/shard_map/dot_general | solution.py:125
  363.5 52.3 %all_to_all.21.blocks_ref = bf16[8,512,512]{2,1,0:T(8,128)(2,1)} all-to-all(bf16[8,512,512]{2,1,0:T(8,128)(2,1)S(1)} %bitcast.105), channel_id=1, replica_groups=mesh['dp'=8,'tensor'=4] {'dp'}, dimensions={0} | all-to-all | bytes 8388608 | tf_op jit(solution)/shard_map/all_to_all | solution.py:132
  415.8 9.1 %unpack.1 = f32[512,2,2048]{2,1,0:T(2,128)} custom-call(bf16[8,512,512]{2,1,0:T(8,128)(2,1)} %all_to_all.21.blocks_ref), custom_call_target="tpu_custom_call" | custom-call | tf_op jit(solution)/shard_map/unpack/pallas_call | solution.py:65
  (25 shorter events, 3.5 us)
Async XLA Ops:
  6.5 4.3 copy-start.3
  6.5 95.5 %all-gather.4.cloned.1.call-start = ((), (), s32[]{:S(2)}) async-start(), calls=%async_computation.4 | async-start | bytes 5242880 | tf_op jit(solution)/shard_map/all_gather | solution.py:88
  16.7 31.8 %all-to-all-start.1 = ((bf16[8,512,256]{2,1,0:T(8,128)(2,1)}), bf16[8,512,256]{2,1,0:T(8,128)(2,1)S(1)}, u32[]{:S(2)}, u32[]{:S(2)}) async-start(bf16[8,512,256]{2,1,0:T(8,128)(2,1)} %bitcast_dynamic-update-slice_fusion), calls=%async_computation.1 | async-start | bytes 4194304 | tf_op jit(solution)/shard_map/all_to_all | solution.py:83
  21.9 230.7 %all-gather.8.cloned.1.call-start = ((), (), s32[]{:S(2)}) async-start(), calls=%async_computation.6 | async-start | bytes 23592960 | tf_op jit(solution)/shard_map/all_gather | solution.py:111
  48.6 76.7 %copy-start = (bf16[8,512,256]{2,1,0:T(8,128)(2,1)}, bf16[8,512,256]{2,1,0:T(8,128)(2,1)S(1)}, u32[]{:S(2)}) copy-start(bf16[8,512,256]{2,1,0:T(8,128)(2,1)S(1)} %all-to-all-done.1) | copy-start | bytes 6291460
  105.6 221.0 %all-gather.6.cloned.1.call-start = ((), (), s32[]{:S(2)}) async-start(), calls=%async_computation.5 | async-start | bytes 14155776 | tf_op jit(solution)/shard_map/all_gather | solution.py:111
  120.1 150.6 %all-to-all-start.2 = ((bf16[8,512,512]{2,1,0:T(8,128)(2,1)}), bf16[8,512,512]{2,1,0:T(8,128)(2,1)}, u32[]{:S(2)}, u32[]{:S(2)}) async-start(bf16[8,512,512]{2,1,0:T(8,128)(2,1)} %fusion.37), calls=%async_computation.2 | async-start | bytes 8388608 | tf_op jit(solution)/shard_map/all_to_all | solution.py:83
  127.1 2.2 slice-start
  288.9 6.3 %copy-start.2 = (f32[2560,512]{0,1:T(8,128)S(1)}, f32[2560,512]{0,1:T(8,128)}, u32[]{:S(2)}) copy-start(f32[2560,512]{0,1:T(8,128)} %fusion.46) | copy-start | bytes 15728644
  337.2 10.7 %copy-start.1 = (f32[1536,256]{0,1:T(8,128)S(1)}, f32[1536,256]{0,1:T(8,128)}, u32[]{:S(2)}) copy-start(f32[1536,256]{0,1:T(8,128)} %copy.10) | copy-start | bytes 4718596
Sparse Core Ops, SparseCore 0:
  10.9 83.4 all-gather.3
  105.7 146.8 all-gather.7
  254.6 71.9 all-gather.5
